TPU v7x, 32 devices: a whole 2x2x4 slice. The times are simulated.
32 devices in a mesh: row: 4 (over x, core), col: 8 (over z, y).
Axes of the slice: x: 2, y: 2, z: 4, core: 2. Of those that a mesh axis runs over, the one named last changes fastest.
Arguments:
- vectors: float32 [8192, 1024], P('row', 'col'), may hold values from -6 to 6
- reflectors: float32 [4, 32, 256, 128], P('row', 'col'), may hold values from -0.375 to 0.375
- wy_factors: float32 [4, 32, 128, 128], P('row', 'col'), may hold values from -1 to 3, as said below
- block_slots: int32 [4, 4, 4], P('row'), may hold values from 0 to 31, as said below
- offsets: int32 [4, 4, 3], P('row'), may hold values from 0 to 1792
Outputs:
- transformed: float32 [8192, 1024], P('row', 'col')
Inputs may be any that keep to these rules, and one draw needn't show every extreme that they name: `wy_factors`: upper triangular; diagonal entries between 1.2 and 2.8. `block_slots`: the entries of one row group are distinct; slot k of every group lies on the col index k // 4. The border entry of the last row group is not read.
All inputs are finite; a program needn't handle non-finite values.
Results may differ from a plain program's by a relative error of at most 0.00026.
Values sent between devices are 32-bit elements; how exact they have to be, the bound alone decides.
No kernel may reach another device: no remote copies, remote signals or barrier semaphores. Data moves between devices by JAX's collectives and lax.ppermute only.
A program may use at most 64 MiB of HBM per device.

v0:
```python
import jax
import jax.numpy as jnp
from jax import lax
from jax.sharding import PartitionSpec as P


def spread(block, axis, source):
    block = jnp.where(lax.axis_index(axis) == source, block, jnp.zeros_like(block))
    return lax.psum(block, axis)


def shifted(block, axis, distance):
    devices = range(lax.axis_size(axis))
    route = [(i - distance, i) for i in devices if i - distance in devices]
    return lax.ppermute(block, axis, route)


def reflect(block, basis, factor):
    best = lax.Precision.HIGHEST
    coeffs = jnp.dot(basis.T, block, precision=best, preferred_element_type=jnp.float32)
    scaled = jnp.dot(factor, coeffs, precision=best, preferred_element_type=jnp.float32)
    return block - jnp.dot(basis, scaled, precision=best, preferred_element_type=jnp.float32)


def fetch_block(block_slots, reflectors, wy_factors, step_no, block_no):
    hold_count = reflectors.shape[1]
    slot_id = block_slots[0, step_no, block_no]
    local_slot = slot_id % hold_count
    root_col = slot_id // hold_count
    parcel = (
        lax.dynamic_index_in_dim(reflectors[0], local_slot, 0, False),
        lax.dynamic_index_in_dim(wy_factors[0], local_slot, 0, False),
    )
    return (spread(parcel[0], "col", root_col), spread(parcel[1], "col", root_col))


def advance(
    current, incoming, beneath, step_no, group_index, group_total_count, bases, factors, offsets
):
    edge_rows = beneath.shape[0]
    total_rows = current.shape[0]
    inner_count = offsets.shape[2]
    head = jnp.where(group_index > 0, incoming, current[:edge_rows])
    current = lax.dynamic_update_slice_in_dim(current, head, 0, 0)
    step_bases = lax.dynamic_index_in_dim(bases, step_no, 0, False)
    step_factors = lax.dynamic_index_in_dim(factors, step_no, 0, False)
    step_offsets = lax.dynamic_index_in_dim(offsets[0], step_no, 0, False)
    for block_no in range(inner_count):
        start = step_offsets[block_no]
        block = lax.dynamic_slice_in_dim(current, start, 2 * edge_rows, 0)
        block = reflect(block, step_bases[block_no], step_factors[block_no])
        current = lax.dynamic_update_slice_in_dim(current, block, start, 0)
    bottom = current[total_rows - edge_rows :]
    joined = reflect(
        jnp.concatenate([bottom, beneath], 0), step_bases[inner_count], step_factors[inner_count]
    )
    has_below = group_index < group_total_count - 1
    tail = jnp.where(has_below, joined[:edge_rows], bottom)
    current = lax.dynamic_update_slice_in_dim(current, tail, total_rows - edge_rows, 0)
    return (current, joined[edge_rows:])


def per_device(vectors, reflectors, wy_factors, block_slots, offsets):
    group_total_count = lax.axis_size("row")
    group_index = lax.axis_index("row")
    step_count = offsets.shape[1]
    inner_count = offsets.shape[2]
    edge_rows = reflectors.shape[3]
    column_count = vectors.shape[1]
    base_list = []
    factor_list = []
    for step_no in range(step_count):
        for block_no in range(inner_count + 1):
            basis, factor = fetch_block(block_slots, reflectors, wy_factors, step_no, block_no)
            base_list.append(basis)
            factor_list.append(factor)
    bases = jnp.stack(base_list).reshape((step_count, inner_count + 1) + base_list[0].shape)
    factors = jnp.stack(factor_list).reshape((step_count, inner_count + 1) + factor_list[0].shape)
    empty_rows = jnp.zeros((edge_rows, column_count), jnp.float32)
    current = vectors

    def wave_tick(tick_no, carry):
        current, incoming = carry
        beneath = shifted(current[:edge_rows], "row", -1)
        time_lag = tick_no - group_index
        step_now = time_lag // 2
        active = (time_lag >= 0) & (time_lag % 2 == 0) & (step_now < step_count)
        step_safe = jnp.clip(step_now, 0, step_count - 1)
        current, outgoing = lax.cond(
            active,
            lambda operands: advance(
                operands[0],
                operands[1],
                beneath,
                step_safe,
                group_index,
                group_total_count,
                bases,
                factors,
                offsets,
            ),
            lambda operands: (operands[0], jnp.zeros_like(operands[1])),
            (current, incoming),
        )
        incoming = shifted(outgoing, "row", 1)
        return (current, incoming)

    current, incoming = lax.fori_loop(
        0, group_total_count + 2 * step_count - 2, wave_tick, (current, empty_rows)
    )
    return current


def solution(mesh):
    in_specs = (
        P("row", "col"),
        P("row", "col", None, None),
        P("row", "col", None, None),
        P("row", None, None),
        P("row", None, None),
    )
    out_specs = P("row", "col")
    return jax.shard_map(
        per_device, mesh=mesh, in_specs=in_specs, out_specs=out_specs, check_vma=False
    )
```

profile of v0, /device:TPU:3, one launch (start us, length us, event | category | flops | bytes accessed | tf_op | source)
XLA Modules:
  0.0 467.7 jit_solution(14436373289902219683)
XLA Ops:
  48.8 1.0 select_bitcast_fusion
  51.6 144.5 %all-reduce.3.cloned.1.call-done = (f32[1,256,128]{2,1,0:T(8,128)}, f32[1,256,128]{2,1,0:T(8,128)}, f32[1,256,128]{2,1,0:T(8,128)}, f32[1,256,128]{2,1,0:T(8,128...) async-done(((f32[1,256,128]{2,1,0:T(8,128)}, ...) | async-done | bytes 3145744 | tf_op jit(solution)/shard_map/psum | solution.py:9
  210.9 249.0 %while.20 = (s32[]{:T(128)}, f32[2048,128]{1,0:T(8,128)S(1)}, f32[128,128]{1,0:T(8,128)S(1)}, s32[]{:T(128)}, s32[1,4,3]{1,0,2:T(1,128)S(1)}, /*index=5*/f32[4,4...) while((s32[]{:T(128)}, f32[2048,128]{1,0:T(8,128)S(1)}, ...), condition=%wide.region_35.36_spmd, body=%wide.region_32.35_spmd.sunk | while | flops 503545888 | bytes 6030164 | solution.py:108
  210.9 2.7 collective-permute-start
  214.5 1.3 collective-permute-start.1
  215.8 2.4 collective-permute-done.1
  218.2 4.9 %collective-permute-start = (f32[128,128]{1,0:T(8,128)S(1)}, f32[128,128]{1,0:T(8,128)S(1)}, u32[]{:S(2)}, u32[]{:S(2)}) collective-permute-start(f32[128,128]{1,0:T(8,128)S(1)} %slice.171), channel_id=1, source_target_pairs={{8,0},{16,8},{24,16},{9,1},{17,9},{25,17},{10,2},{18,10},{26,18},{... | collective-permute-start | bytes 196616 | tf_op jit(solution)/shard_map/while/body/eval_jaxpr/ppermute | solution.py:15
  224.0 1.3 collective-permute-start.1
  225.2 14.7 %collective-permute-done.1 = f32[128,128]{1,0:T(8,128)S(1)} collective-permute-done((f32[128,128]{1,0:T(8,128)S(1)}, f32[128,128]{1,0:T(8,128)S(1)}, u32[]{:S(2)}, u32[]{:S(2)}) %collective-permute-start.1) | collective-permute-done | bytes 65568 | tf_op jit(solution)/shard_map/while/body/eval_jaxpr/ppermute | solution.py:15
  240.0 21.1 %collective-permute-start = (f32[128,128]{1,0:T(8,128)S(1)}, f32[128,128]{1,0:T(8,128)S(1)}, u32[]{:S(2)}, u32[]{:S(2)}) collective-permute-start(f32[128,128]{1,0:T(8,128)S(1)} %slice.171), channel_id=1, source_target_pairs={{8,0},{16,8},{24,16},{9,1},{17,9},{25,17},{10,2},{18,10},{26,18},{... | collective-permute-start | bytes 196616 | tf_op jit(solution)/shard_map/while/body/eval_jaxpr/ppermute | solution.py:15
  262.0 1.3 collective-permute-start.1
  263.3 18.3 %collective-permute-done.1 = f32[128,128]{1,0:T(8,128)S(1)} collective-permute-done((f32[128,128]{1,0:T(8,128)S(1)}, f32[128,128]{1,0:T(8,128)S(1)}, u32[]{:S(2)}, u32[]{:S(2)}) %collective-permute-start.1) | collective-permute-done | bytes 65568 | tf_op jit(solution)/shard_map/while/body/eval_jaxpr/ppermute | solution.py:15
  281.5 4.8 %collective-permute-start = (f32[128,128]{1,0:T(8,128)S(1)}, f32[128,128]{1,0:T(8,128)S(1)}, u32[]{:S(2)}, u32[]{:S(2)}) collective-permute-start(f32[128,128]{1,0:T(8,128)S(1)} %slice.171), channel_id=1, source_target_pairs={{8,0},{16,8},{24,16},{9,1},{17,9},{25,17},{10,2},{18,10},{26,18},{... | collective-permute-start | bytes 196616 | tf_op jit(solution)/shard_map/while/body/eval_jaxpr/ppermute | solution.py:15
  287.3 16.2 %conditional.2 = (f32[2048,128]{1,0:T(8,128)S(1)}, f32[128,128]{1,0:T(8,128)S(1)}) conditional(s32[]{:T(128)} %convert_element_type.11, f32[2048,128]{1,0:T(8,128)S(1)} %get-tuple-element.402, (s32[]{:T(128)}, f32[2048,128]{1,0:T(8,128)S(1)}, f32[128,128]{1,0:T(8,128)S(1)}, s32[]{:T(128)}, s32[1,4,3]{1,0,2:T(1,128)S(1)}, ...), branch_computations={%region_33.33_spmd, %region_34.34_spmd} | conditional | flops 503545856 | bytes 5374306 | solution.py:89
  290.1 1.0 fusion.11
  291.4 1.0 dynamic_update_slice.16
  294.7 1.0 fusion.10
  296.0 1.0 dynamic_update_slice.17
  299.3 1.0 fusion.9
  300.6 1.0 dynamic_update_slice.18
  302.1 1.0 fusion.8
  303.5 1.3 collective-permute-start.1
  304.8 1.8 collective-permute-done.1
  306.6 5.4 %collective-permute-start = (f32[128,128]{1,0:T(8,128)S(1)}, f32[128,128]{1,0:T(8,128)S(1)}, u32[]{:S(2)}, u32[]{:S(2)}) collective-permute-start(f32[128,128]{1,0:T(8,128)S(1)} %slice.171), channel_id=1, source_target_pairs={{8,0},{16,8},{24,16},{9,1},{17,9},{25,17},{10,2},{18,10},{26,18},{... | collective-permute-start | bytes 196616 | tf_op jit(solution)/shard_map/while/body/eval_jaxpr/ppermute | solution.py:15
  312.9 1.3 collective-permute-start.1
  314.2 18.6 %collective-permute-done.1 = f32[128,128]{1,0:T(8,128)S(1)} collective-permute-done((f32[128,128]{1,0:T(8,128)S(1)}, f32[128,128]{1,0:T(8,128)S(1)}, u32[]{:S(2)}, u32[]{:S(2)}) %collective-permute-start.1) | collective-permute-done | bytes 65568 | tf_op jit(solution)/shard_map/while/body/eval_jaxpr/ppermute | solution.py:15
  332.8 4.8 %collective-permute-start = (f32[128,128]{1,0:T(8,128)S(1)}, f32[128,128]{1,0:T(8,128)S(1)}, u32[]{:S(2)}, u32[]{:S(2)}) collective-permute-start(f32[128,128]{1,0:T(8,128)S(1)} %slice.171), channel_id=1, source_target_pairs={{8,0},{16,8},{24,16},{9,1},{17,9},{25,17},{10,2},{18,10},{26,18},{... | collective-permute-start | bytes 196616 | tf_op jit(solution)/shard_map/while/body/eval_jaxpr/ppermute | solution.py:15
  338.5 15.9 %conditional.2 = (f32[2048,128]{1,0:T(8,128)S(1)}, f32[128,128]{1,0:T(8,128)S(1)}) conditional(s32[]{:T(128)} %convert_element_type.11, f32[2048,128]{1,0:T(8,128)S(1)} %get-tuple-element.402, (s32[]{:T(128)}, f32[2048,128]{1,0:T(8,128)S(1)}, f32[128,128]{1,0:T(8,128)S(1)}, s32[]{:T(128)}, s32[1,4,3]{1,0,2:T(1,128)S(1)}, ...), branch_computations={%region_33.33_spmd, %region_34.34_spmd} | conditional | flops 503545856 | bytes 5374306 | solution.py:89
  341.3 1.0 fusion.11
  342.6 1.0 dynamic_update_slice.16
  346.0 1.0 fusion.10
  347.3 1.0 dynamic_update_slice.17
  350.6 1.0 fusion.9
  353.0 1.0 fusion.8
  354.4 1.3 collective-permute-start.1
  355.7 1.8 collective-permute-done.1
  357.6 5.7 %collective-permute-start = (f32[128,128]{1,0:T(8,128)S(1)}, f32[128,128]{1,0:T(8,128)S(1)}, u32[]{:S(2)}, u32[]{:S(2)}) collective-permute-start(f32[128,128]{1,0:T(8,128)S(1)} %slice.171), channel_id=1, source_target_pairs={{8,0},{16,8},{24,16},{9,1},{17,9},{25,17},{10,2},{18,10},{26,18},{... | collective-permute-start | bytes 196616 | tf_op jit(solution)/shard_map/while/body/eval_jaxpr/ppermute | solution.py:15
  364.1 1.3 collective-permute-start.1
  365.4 18.2 %collective-permute-done.1 = f32[128,128]{1,0:T(8,128)S(1)} collective-permute-done((f32[128,128]{1,0:T(8,128)S(1)}, f32[128,128]{1,0:T(8,128)S(1)}, u32[]{:S(2)}, u32[]{:S(2)}) %collective-permute-start.1) | collective-permute-done | bytes 65568 | tf_op jit(solution)/shard_map/while/body/eval_jaxpr/ppermute | solution.py:15
  383.6 4.8 %collective-permute-start = (f32[128,128]{1,0:T(8,128)S(1)}, f32[128,128]{1,0:T(8,128)S(1)}, u32[]{:S(2)}, u32[]{:S(2)}) collective-permute-start(f32[128,128]{1,0:T(8,128)S(1)} %slice.171), channel_id=1, source_target_pairs={{8,0},{16,8},{24,16},{9,1},{17,9},{25,17},{10,2},{18,10},{26,18},{... | collective-permute-start | bytes 196616 | tf_op jit(solution)/shard_map/while/body/eval_jaxpr/ppermute | solution.py:15
  389.3 15.8 %conditional.2 = (f32[2048,128]{1,0:T(8,128)S(1)}, f32[128,128]{1,0:T(8,128)S(1)}) conditional(s32[]{:T(128)} %convert_element_type.11, f32[2048,128]{1,0:T(8,128)S(1)} %get-tuple-element.402, (s32[]{:T(128)}, f32[2048,128]{1,0:T(8,128)S(1)}, f32[128,128]{1,0:T(8,128)S(1)}, s32[]{:T(128)}, s32[1,4,3]{1,0,2:T(1,128)S(1)}, ...), branch_computations={%region_33.33_spmd, %region_34.34_spmd} | conditional | flops 503545856 | bytes 5374306 | solution.py:89
  392.1 1.0 fusion.11
  393.5 1.0 dynamic_update_slice.16
  396.8 1.0 fusion.10
  401.0 1.0 fusion.9
  402.3 1.0 dynamic_update_slice.18
  403.8 1.0 fusion.8
  405.1 1.3 collective-permute-start.1
  406.4 1.8 collective-permute-done.1
  408.3 5.8 %collective-permute-start = (f32[128,128]{1,0:T(8,128)S(1)}, f32[128,128]{1,0:T(8,128)S(1)}, u32[]{:S(2)}, u32[]{:S(2)}) collective-permute-start(f32[128,128]{1,0:T(8,128)S(1)} %slice.171), channel_id=1, source_target_pairs={{8,0},{16,8},{24,16},{9,1},{17,9},{25,17},{10,2},{18,10},{26,18},{... | collective-permute-start | bytes 196616 | tf_op jit(solution)/shard_map/while/body/eval_jaxpr/ppermute | solution.py:15
  415.0 1.3 collective-permute-start.1
  416.3 18.6 %collective-permute-done.1 = f32[128,128]{1,0:T(8,128)S(1)} collective-permute-done((f32[128,128]{1,0:T(8,128)S(1)}, f32[128,128]{1,0:T(8,128)S(1)}, u32[]{:S(2)}, u32[]{:S(2)}) %collective-permute-start.1) | collective-permute-done | bytes 65568 | tf_op jit(solution)/shard_map/while/body/eval_jaxpr/ppermute | solution.py:15
  434.8 4.8 %collective-permute-start = (f32[128,128]{1,0:T(8,128)S(1)}, f32[128,128]{1,0:T(8,128)S(1)}, u32[]{:S(2)}, u32[]{:S(2)}) collective-permute-start(f32[128,128]{1,0:T(8,128)S(1)} %slice.171), channel_id=1, source_target_pairs={{8,0},{16,8},{24,16},{9,1},{17,9},{25,17},{10,2},{18,10},{26,18},{... | collective-permute-start | bytes 196616 | tf_op jit(solution)/shard_map/while/body/eval_jaxpr/ppermute | solution.py:15
  440.6 16.2 %conditional.2 = (f32[2048,128]{1,0:T(8,128)S(1)}, f32[128,128]{1,0:T(8,128)S(1)}) conditional(s32[]{:T(128)} %convert_element_type.11, f32[2048,128]{1,0:T(8,128)S(1)} %get-tuple-element.402, (s32[]{:T(128)}, f32[2048,128]{1,0:T(8,128)S(1)}, f32[128,128]{1,0:T(8,128)S(1)}, s32[]{:T(128)}, s32[1,4,3]{1,0,2:T(1,128)S(1)}, ...), branch_computations={%region_33.33_spmd, %region_34.34_spmd} | conditional | flops 503545856 | bytes 5374306 | solution.py:89
  443.4 1.0 fusion.11
  444.7 1.0 dynamic_update_slice.16
  448.0 1.0 fusion.10
  449.3 1.0 dynamic_update_slice.17
  452.6 1.0 fusion.9
  453.9 1.0 dynamic_update_slice.18
  455.4 1.0 fusion.8
  456.7 1.3 collective-permute-start.1
  458.0 1.8 collective-permute-done.1
  459.9 1.0 copy-done
  (168 shorter events, 41.7 us)
Async XLA Ops:
  6.5 42.2 %copy-start.2 = (f32[1,4,256,128]{3,2,1,0:T(8,128)S(1)}, f32[1,4,256,128]{3,2,1,0:T(8,128)}, u32[]{:S(2)}) copy-start(f32[1,4,256,128]{3,2,1,0:T(8,128)} %param.10) | copy-start | bytes 1572868
  6.5 41.4 %copy-start.3 = (f32[1,4,128,128]{3,2,1,0:T(8,128)S(1)}, f32[1,4,128,128]{3,2,1,0:T(8,128)}, u32[]{:S(2)}) copy-start(f32[1,4,128,128]{3,2,1,0:T(8,128)} %param.11) | copy-start | bytes 786436
  6.5 0.8 copy-start.23
  6.5 189.5 %all-reduce.3.cloned.1.call-start = ((), (), s32[]{:S(2)}) async-start(), calls=%async_computation | async-start | bytes 6291456 | tf_op jit(solution)/shard_map/psum | solution.py:9
  196.1 13.2 %copy-start.21 = (f32[1,128,128]{2,1,0:T(8,128)S(1)}, f32[1,128,128]{2,1,0:T(8,128)}, u32[]{:S(2)}) copy-start(f32[1,128,128]{2,1,0:T(8,128)} %get-tuple-element.283) | copy-start | bytes 196612
  196.1 13.2 %copy-start.20 = (f32[1,128,128]{2,1,0:T(8,128)S(1)}, f32[1,128,128]{2,1,0:T(8,128)}, u32[]{:S(2)}) copy-start(f32[1,128,128]{2,1,0:T(8,128)} %get-tuple-element.284) | copy-start | bytes 196612
  196.1 13.2 %copy-start.19 = (f32[1,256,128]{2,1,0:T(8,128)S(1)}, f32[1,256,128]{2,1,0:T(8,128)}, u32[]{:S(2)}) copy-start(f32[1,256,128]{2,1,0:T(8,128)} %get-tuple-element.254) | copy-start | bytes 393220
  196.1 13.3 %copy-start.18 = (f32[1,256,128]{2,1,0:T(8,128)S(1)}, f32[1,256,128]{2,1,0:T(8,128)}, u32[]{:S(2)}) copy-start(f32[1,256,128]{2,1,0:T(8,128)} %get-tuple-element.255) | copy-start | bytes 393220
  196.1 13.3 %copy-start.17 = (f32[1,256,128]{2,1,0:T(8,128)S(1)}, f32[1,256,128]{2,1,0:T(8,128)}, u32[]{:S(2)}) copy-start(f32[1,256,128]{2,1,0:T(8,128)} %get-tuple-element.256) | copy-start | bytes 393220
  196.1 13.3 %copy-start.16 = (f32[1,256,128]{2,1,0:T(8,128)S(1)}, f32[1,256,128]{2,1,0:T(8,128)}, u32[]{:S(2)}) copy-start(f32[1,256,128]{2,1,0:T(8,128)} %get-tuple-element.257) | copy-start | bytes 393220
  196.1 13.3 %copy-start.15 = (f32[1,256,128]{2,1,0:T(8,128)S(1)}, f32[1,256,128]{2,1,0:T(8,128)}, u32[]{:S(2)}) copy-start(f32[1,256,128]{2,1,0:T(8,128)} %get-tuple-element.258) | copy-start | bytes 393220
  196.1 13.4 %copy-start.14 = (f32[1,256,128]{2,1,0:T(8,128)S(1)}, f32[1,256,128]{2,1,0:T(8,128)}, u32[]{:S(2)}) copy-start(f32[1,256,128]{2,1,0:T(8,128)} %get-tuple-element.259) | copy-start | bytes 393220
  196.1 13.4 %copy-start.13 = (f32[1,256,128]{2,1,0:T(8,128)S(1)}, f32[1,256,128]{2,1,0:T(8,128)}, u32[]{:S(2)}) copy-start(f32[1,256,128]{2,1,0:T(8,128)} %get-tuple-element.260) | copy-start | bytes 393220
  196.1 13.4 %copy-start.12 = (f32[1,256,128]{2,1,0:T(8,128)S(1)}, f32[1,256,128]{2,1,0:T(8,128)}, u32[]{:S(2)}) copy-start(f32[1,256,128]{2,1,0:T(8,128)} %get-tuple-element.261) | copy-start | bytes 393220
  198.0 11.6 %copy-start.11 = (f32[1,256,128]{2,1,0:T(8,128)S(1)}, f32[1,256,128]{2,1,0:T(8,128)}, u32[]{:S(2)}) copy-start(f32[1,256,128]{2,1,0:T(8,128)} %get-tuple-element.262) | copy-start | bytes 393220
  198.9 10.7 %copy-start.10 = (f32[1,256,128]{2,1,0:T(8,128)S(1)}, f32[1,256,128]{2,1,0:T(8,128)}, u32[]{:S(2)}) copy-start(f32[1,256,128]{2,1,0:T(8,128)} %get-tuple-element.263) | copy-start | bytes 393220
  200.6 9.0 %copy-start.9 = (f32[1,256,128]{2,1,0:T(8,128)S(1)}, f32[1,256,128]{2,1,0:T(8,128)}, u32[]{:S(2)}) copy-start(f32[1,256,128]{2,1,0:T(8,128)} %get-tuple-element.264) | copy-start | bytes 393220
  202.3 7.3 %copy-start.8 = (f32[1,256,128]{2,1,0:T(8,128)S(1)}, f32[1,256,128]{2,1,0:T(8,128)}, u32[]{:S(2)}) copy-start(f32[1,256,128]{2,1,0:T(8,128)} %get-tuple-element.265) | copy-start | bytes 393220
  204.1 5.6 %copy-start.7 = (f32[1,256,128]{2,1,0:T(8,128)S(1)}, f32[1,256,128]{2,1,0:T(8,128)}, u32[]{:S(2)}) copy-start(f32[1,256,128]{2,1,0:T(8,128)} %get-tuple-element.266) | copy-start | bytes 393220
  205.8 3.9 copy-start.6
  207.5 2.2 copy-start.5
  209.3 1.6 copy-start.1
  209.3 1.6 copy-start.22
  209.3 1.0 copy-start.4
  210.9 3.6 collective-permute-start
  214.5 3.7 collective-permute-start.1
  218.2 5.8 %collective-permute-start = (f32[128,128]{1,0:T(8,128)S(1)}, f32[128,128]{1,0:T(8,128)S(1)}, u32[]{:S(2)}, u32[]{:S(2)}) collective-permute-start(f32[128,128]{1,0:T(8,128)S(1)} %slice.171), channel_id=1, source_target_pairs={{8,0},{16,8},{24,16},{9,1},{17,9},{25,17},{10,2},{18,10},{26,18},{... | collective-permute-start | bytes 196616 | tf_op jit(solution)/shard_map/while/body/eval_jaxpr/ppermute | solution.py:15
  224.0 16.0 %collective-permute-start.1 = (f32[128,128]{1,0:T(8,128)S(1)}, f32[128,128]{1,0:T(8,128)S(1)}, u32[]{:S(2)}, u32[]{:S(2)}) collective-permute-start(f32[128,128]{1,0:T(8,128)S(1)} %get-tuple-element.384), channel_id=1, source_target_pairs={{0,8},{8,16},{16,24},{1,9},{9,17},{17,25},{2,10},{10,18},{18,26},{... | collective-permute-start | bytes 196616 | tf_op jit(solution)/shard_map/while/body/eval_jaxpr/ppermute | solution.py:15
  240.0 22.0 %collective-permute-start = (f32[128,128]{1,0:T(8,128)S(1)}, f32[128,128]{1,0:T(8,128)S(1)}, u32[]{:S(2)}, u32[]{:S(2)}) collective-permute-start(f32[128,128]{1,0:T(8,128)S(1)} %slice.171), channel_id=1, source_target_pairs={{8,0},{16,8},{24,16},{9,1},{17,9},{25,17},{10,2},{18,10},{26,18},{... | collective-permute-start | bytes 196616 | tf_op jit(solution)/shard_map/while/body/eval_jaxpr/ppermute | solution.py:15
  262.0 19.6 %collective-permute-start.1 = (f32[128,128]{1,0:T(8,128)S(1)}, f32[128,128]{1,0:T(8,128)S(1)}, u32[]{:S(2)}, u32[]{:S(2)}) collective-permute-start(f32[128,128]{1,0:T(8,128)S(1)} %get-tuple-element.384), channel_id=1, source_target_pairs={{0,8},{8,16},{16,24},{1,9},{9,17},{17,25},{2,10},{10,18},{18,26},{... | collective-permute-start | bytes 196616 | tf_op jit(solution)/shard_map/while/body/eval_jaxpr/ppermute | solution.py:15
  281.5 5.7 %collective-permute-start = (f32[128,128]{1,0:T(8,128)S(1)}, f32[128,128]{1,0:T(8,128)S(1)}, u32[]{:S(2)}, u32[]{:S(2)}) collective-permute-start(f32[128,128]{1,0:T(8,128)S(1)} %slice.171), channel_id=1, source_target_pairs={{8,0},{16,8},{24,16},{9,1},{17,9},{25,17},{10,2},{18,10},{26,18},{... | collective-permute-start | bytes 196616 | tf_op jit(solution)/shard_map/while/body/eval_jaxpr/ppermute | solution.py:15
  303.5 3.1 collective-permute-start.1
  306.6 6.3 %collective-permute-start = (f32[128,128]{1,0:T(8,128)S(1)}, f32[128,128]{1,0:T(8,128)S(1)}, u32[]{:S(2)}, u32[]{:S(2)}) collective-permute-start(f32[128,128]{1,0:T(8,128)S(1)} %slice.171), channel_id=1, source_target_pairs={{8,0},{16,8},{24,16},{9,1},{17,9},{25,17},{10,2},{18,10},{26,18},{... | collective-permute-start | bytes 196616 | tf_op jit(solution)/shard_map/while/body/eval_jaxpr/ppermute | solution.py:15
  312.9 19.9 %collective-permute-start.1 = (f32[128,128]{1,0:T(8,128)S(1)}, f32[128,128]{1,0:T(8,128)S(1)}, u32[]{:S(2)}, u32[]{:S(2)}) collective-permute-start(f32[128,128]{1,0:T(8,128)S(1)} %get-tuple-element.384), channel_id=1, source_target_pairs={{0,8},{8,16},{16,24},{1,9},{9,17},{17,25},{2,10},{10,18},{18,26},{... | collective-permute-start | bytes 196616 | tf_op jit(solution)/shard_map/while/body/eval_jaxpr/ppermute | solution.py:15
  332.8 5.7 %collective-permute-start = (f32[128,128]{1,0:T(8,128)S(1)}, f32[128,128]{1,0:T(8,128)S(1)}, u32[]{:S(2)}, u32[]{:S(2)}) collective-permute-start(f32[128,128]{1,0:T(8,128)S(1)} %slice.171), channel_id=1, source_target_pairs={{8,0},{16,8},{24,16},{9,1},{17,9},{25,17},{10,2},{18,10},{26,18},{... | collective-permute-start | bytes 196616 | tf_op jit(solution)/shard_map/while/body/eval_jaxpr/ppermute | solution.py:15
  354.4 3.1 collective-permute-start.1
  357.6 6.6 %collective-permute-start = (f32[128,128]{1,0:T(8,128)S(1)}, f32[128,128]{1,0:T(8,128)S(1)}, u32[]{:S(2)}, u32[]{:S(2)}) collective-permute-start(f32[128,128]{1,0:T(8,128)S(1)} %slice.171), channel_id=1, source_target_pairs={{8,0},{16,8},{24,16},{9,1},{17,9},{25,17},{10,2},{18,10},{26,18},{... | collective-permute-start | bytes 196616 | tf_op jit(solution)/shard_map/while/body/eval_jaxpr/ppermute | solution.py:15
  364.1 19.5 %collective-permute-start.1 = (f32[128,128]{1,0:T(8,128)S(1)}, f32[128,128]{1,0:T(8,128)S(1)}, u32[]{:S(2)}, u32[]{:S(2)}) collective-permute-start(f32[128,128]{1,0:T(8,128)S(1)} %get-tuple-element.384), channel_id=1, source_target_pairs={{0,8},{8,16},{16,24},{1,9},{9,17},{17,25},{2,10},{10,18},{18,26},{... | collective-permute-start | bytes 196616 | tf_op jit(solution)/shard_map/while/body/eval_jaxpr/ppermute | solution.py:15
  383.6 5.7 %collective-permute-start = (f32[128,128]{1,0:T(8,128)S(1)}, f32[128,128]{1,0:T(8,128)S(1)}, u32[]{:S(2)}, u32[]{:S(2)}) collective-permute-start(f32[128,128]{1,0:T(8,128)S(1)} %slice.171), channel_id=1, source_target_pairs={{8,0},{16,8},{24,16},{9,1},{17,9},{25,17},{10,2},{18,10},{26,18},{... | collective-permute-start | bytes 196616 | tf_op jit(solution)/shard_map/while/body/eval_jaxpr/ppermute | solution.py:15
  405.1 3.1 collective-permute-start.1
  408.3 6.7 %collective-permute-start = (f32[128,128]{1,0:T(8,128)S(1)}, f32[128,128]{1,0:T(8,128)S(1)}, u32[]{:S(2)}, u32[]{:S(2)}) collective-permute-start(f32[128,128]{1,0:T(8,128)S(1)} %slice.171), channel_id=1, source_target_pairs={{8,0},{16,8},{24,16},{9,1},{17,9},{25,17},{10,2},{18,10},{26,18},{... | collective-permute-start | bytes 196616 | tf_op jit(solution)/shard_map/while/body/eval_jaxpr/ppermute | solution.py:15
  415.0 19.9 %collective-permute-start.1 = (f32[128,128]{1,0:T(8,128)S(1)}, f32[128,128]{1,0:T(8,128)S(1)}, u32[]{:S(2)}, u32[]{:S(2)}) collective-permute-start(f32[128,128]{1,0:T(8,128)S(1)} %get-tuple-element.384), channel_id=1, source_target_pairs={{0,8},{8,16},{16,24},{1,9},{9,17},{17,25},{2,10},{10,18},{18,26},{... | collective-permute-start | bytes 196616 | tf_op jit(solution)/shard_map/while/body/eval_jaxpr/ppermute | solution.py:15
  434.8 5.7 %collective-permute-start = (f32[128,128]{1,0:T(8,128)S(1)}, f32[128,128]{1,0:T(8,128)S(1)}, u32[]{:S(2)}, u32[]{:S(2)}) collective-permute-start(f32[128,128]{1,0:T(8,128)S(1)} %slice.171), channel_id=1, source_target_pairs={{8,0},{16,8},{24,16},{9,1},{17,9},{25,17},{10,2},{18,10},{26,18},{... | collective-permute-start | bytes 196616 | tf_op jit(solution)/shard_map/while/body/eval_jaxpr/ppermute | solution.py:15
  456.7 3.1 collective-permute-start.1
  459.9 1.0 copy-start
Sparse Core Ops, SparseCore 0:
  51.7 144.3 all-reduce.2
where the time goes:
time: 470 us; the launch traced here: 468 us
  waiting for transfers between devices  251 us (53%)
  starting transfers between devices  77.7 us (17%)
  between operations  53.7 us (11%)
  local copies, waits for them, and re-layouts  31 us (7%)
  matrix products  27.3 us (6%)
  loops' own time  23.2 us (5%)
    psum x1, waiting for transfers between devices, spread(): return lax.psum(block, axis)  144 us
    ppermute x20, waiting for transfers between devices, shifted(): return lax.ppermute(block, axis, route)  106 us
    ppermute x20, starting transfers between devices, shifted(): return lax.ppermute(block, axis, route)  77.7 us
    another operation x10, loops' own time, wave_tick(): lax.cond(active, lambda operands: advance(operands[0], operands[1], benea...  22.5 us
    dot_general x16, matrix products, reflect(): jnp.dot(factor, coeffs, precision=best, preferred_element_type=jnp.float32)  16.8 us
    unnamed x78, local copies, waits for them, and re-layouts  16.1 us
    dynamic_update_slice x12, local copies, waits for them, and re-layouts, advance(): current = lax.dynamic_update_slice_in_dim(current, block, start, 0)  11.5 us
  transfers between devices with their start and end apart: 21, of which 21 were waited for; matrix products, arithmetic and copies ran while one was open for 0% of the time, Pallas kernels for 0%

commit v1 on v0

v1 whole, which is shorter than its diff:
```python
import functools
import math

import jax
import jax.numpy as jnp
from jax import lax
from jax.experimental import pallas as pl
from jax.experimental.pallas import tpu as pltpu
from jax.sharding import PartitionSpec as P

F32 = jnp.float32
BF16 = jnp.bfloat16


def split(x):
    high = x.astype(BF16)
    return high, (x - high.astype(F32)).astype(BF16)


def product(a, b, dims=(((1,), (0,)), ((), ()))):
    dot = functools.partial(lax.dot_general, dimension_numbers=dims, preferred_element_type=F32)
    return dot(a[0], b[0]) + (dot(a[0], b[1]) + dot(a[1], b[0]))


def ring_pairs(count, stride_of):
    return [(i, stride_of(i)) for i in range(count)]


def gather_pieces(piece, n_col, n_y):
    n_z = n_col // n_y
    me = lax.axis_index("col")
    z, y = me // n_y, me % n_y
    forward = ring_pairs(n_col, lambda i: (i + n_y) % n_col)
    backward = ring_pairs(n_col, lambda i: (i - n_y) % n_col)
    turn = ring_pairs(n_col, lambda i: i // n_y * n_y + (i % n_y + 1) % n_y)
    found = []

    def spread_y(block, dz, parts):
        sent = block
        for dy in range(1, n_y):
            sent = lax.ppermute(sent, "col", turn)
            for part, z_back in parts:
                source = (z - z_back) % n_z * n_y + (y - dy) % n_y
                found.append((sent[part], source))

    found.append((piece, me))
    count = piece.shape[0]
    low, high = piece, piece
    whole = slice(0, count)
    arrivals = [(piece, 0, [(whole, 0)])]
    for step in range(1, n_z // 2 + 1):
        if 2 * step == n_z:
            cut = count // 2
            far = jnp.concatenate(
                [lax.ppermute(low[:cut], "col", backward), lax.ppermute(high[cut:], "col", forward)], 0
            )
            found.append((far, (z - step) % n_z * n_y + y))
            arrivals.append((far, step, [(whole, step)]))
        else:
            low = lax.ppermute(low, "col", backward)
            high = lax.ppermute(high, "col", forward)
            found.append((low, (z + step) % n_z * n_y + y))
            found.append((high, (z - step) % n_z * n_y + y))
            arrivals.append((low, -step, [(whole, -step)]))
            arrivals.append((high, step, [(whole, step)]))
    for block, dz, parts in arrivals:
        spread_y(block, dz, parts)
    return found


def exchange_slots(reflectors, wy_factors, block_slots, n_col):
    hold, rows, width = reflectors.shape
    parcels = jnp.concatenate(
        [reflectors.reshape(hold, n_col, -1, width), wy_factors.reshape(hold, n_col, -1, width)], 2
    ).transpose(1, 0, 2, 3)
    parcels = lax.all_to_all(parcels, "col", 0, 0, tiled=True)
    parcels = parcels.reshape((n_col * hold,) + parcels.shape[2:])
    slots = jnp.clip(block_slots.reshape(-1), 0, n_col * hold - 1)
    return jnp.take(parcels, slots, axis=0)


def prepare_kernel(rows, width, sources, *refs):
    n = (len(refs) - 3)
    pieces, out, edge, t_scr = refs[:n], refs[n], refs[n + 1], refs[n + 2]
    v_rows, t_rows = rows // n, width // n
    per_step = out.shape[0]
    for b in range(per_step):
        for i in range(n):
            at = sources[i]
            out[b, pl.ds(pl.multiple_of(at * v_rows, v_rows), v_rows), :] = pieces[i][b, :v_rows, :]
            t_scr[b, pl.ds(pl.multiple_of(at * t_rows, t_rows), t_rows), :] = pieces[i][b, v_rows:, :]
    for b in range(per_step):
        basis = out[b, :rows, :]
        z = product(split(t_scr[b]), split(basis), (((1,), (1,)), ((), ())))
        out[b, rows : rows + width, :] = z[:, :width]
        out[b, rows + width :, :] = z[:, width:]
    edge[0, :width, :] = out[per_step - 1, width:rows, :]
    edge[0, width:, :] = out[per_step - 1, rows + width :, :]


def prepare(found, rows, width, steps):
    blocks = found[0][0].shape[0]
    per_step = blocks // steps
    n = len(found)
    v_rows, t_rows = rows // n, width // n
    if t_rows % 8:
        order = jnp.stack([source for _, source in found])
        stacked = jnp.stack([piece for piece, _ in found])
        stacked = jnp.take(stacked, jnp.argsort(order), axis=0).transpose(1, 0, 2, 3)
        found = [
            (
                jnp.concatenate(
                    [
                        stacked[:, :, :v_rows].reshape(blocks, rows, width),
                        stacked[:, :, v_rows:].reshape(blocks, width, width),
                    ],
                    1,
                ),
                jnp.int32(0),
            )
        ]
        n, v_rows, t_rows = 1, rows, width
    sources = jnp.stack([source for _, source in found]).astype(jnp.int32)
    return pl.pallas_call(
        functools.partial(prepare_kernel, rows, width),
        grid_spec=pltpu.PrefetchScalarGridSpec(
            num_scalar_prefetch=1,
            grid=(steps,),
            in_specs=[pl.BlockSpec((per_step, v_rows + t_rows, width), lambda s, _: (s, 0, 0))] * n,
            out_specs=[
                pl.BlockSpec((per_step, 2 * rows, width), lambda s, _: (s, 0, 0)),
                pl.BlockSpec((1, 2 * width, width), lambda s, _: (s, 0, 0)),
            ],
            scratch_shapes=[pltpu.VMEM((per_step, width, width), F32)],
        ),
        out_shape=[
            jax.ShapeDtypeStruct((blocks, 2 * rows, width), F32),
            jax.ShapeDtypeStruct((steps, 2 * width, width), F32),
        ],
        name="prepare",
    )(sources, *[piece for piece, _ in found])


def wave_kernel(plan, *refs):
    ticks, first, last, steps, inner, pairs, n_links = plan
    refs = list(refs)
    offs, place = refs.pop(0), refs.pop(0)
    x_in = [refs.pop(0), refs.pop(0)]
    vz = [refs.pop(0), refs.pop(0)]
    prev = [refs.pop(0), refs.pop(0)]
    if first:
        mine = [refs.pop(0) for _ in range(n_links)]
        theirs = [refs.pop(0) for _ in range(n_links)]
    x = [refs.pop(0), refs.pop(0)]
    out = refs
    p, k = place[0], place[1]
    per_step = inner + 1
    total_rows = x[0].shape[0]
    width = vz[0].shape[2]
    rows = 2 * width
    for h in range(2):
        x[h][...] = x_in[h][...]

    def valid(step):
        return (step >= 0) & (step < steps), jnp.clip(step, 0, steps - 1)

    def pick(cond, a, b):
        return jnp.where(cond, a, b)

    def down(tick):
        act, step = valid(tick - 2 * p - 1)
        block = step * per_step + inner
        is_own = k == 1
        v = pick(is_own, vz[0][block, :width, :], vz[1][block, :width, :])
        z = pick(is_own, vz[0][block, rows : rows + width, :], vz[1][block, rows : rows + width, :])
        return act & (p < pairs - 1), total_rows - width, is_own, v, z

    def up(tick):
        act, step = valid(tick - 2 * p + 1)
        v = pick(k == 0, prev[0][step, :width, :], prev[1][step, :width, :])
        z = pick(k == 0, prev[0][step, width:, :], prev[1][step, width:, :])
        return act & (p > 0), 0, k == 0, v, z

    def links(tick):
        if n_links == 2:
            return [down(tick), up(tick)]
        a, b = down(tick), up(tick)
        c = p == 0
        row = pl.multiple_of(jnp.where(c, a[1], b[1]), width)
        return [(pick(c, a[0], b[0]), row, pick(c, a[2], b[2]), pick(c, a[3], b[3]), pick(c, a[4], b[4]))]

    if first:
        for (act, row, is_own, v, _), a, b in zip(links(ticks[0] - 1), mine, theirs):
            delta = product(split(v), split(pick(act, a[...] + b[...], 0.0)))
            for h, mask in ((0, is_own), (1, jnp.logical_not(is_own))):
                at = pl.ds(row, width)
                x[h][at, :] = x[h][at, :] - pick(mask, delta, 0.0)

    for tick in ticks:
        for j in range(inner):
            for h in range(2):
                group = k if h == 0 else 1 - k
                act, step = valid(tick - 2 * p - group)
                start = offs[h, step * inner + j]
                block = step * per_step + j
                at = pl.ds(start, rows)
                xb = x[h][at, :]
                z = jnp.concatenate([vz[h][block, rows : rows + width, :], vz[h][block, rows + width :, :]], 1)
                y = pick(act, product(split(z), split(xb)), 0.0)
                x[h][at, :] = xb - product(split(vz[h][block, :rows, :]), split(y))
        if last and tick == ticks[-1]:
            for (act, row, is_own, _, z), o in zip(links(tick), out):
                at = pl.ds(row, width)
                edge = pick(is_own, x[0][at, :], x[1][at, :])
                o[...] = pick(act, product(split(z), split(edge)), 0.0)
        act, step = valid(tick - 2 * p)
        block = step * per_step + inner
        is_own = k == 0
        halves = []
        for h in range(2):
            lo, hi = (0, width) if h == 0 else (width, 0)
            v = pick(is_own, vz[0][block, lo : lo + width, :], vz[1][block, hi : hi + width, :])
            z = pick(
                is_own,
                vz[0][block, rows + lo : rows + lo + width, :],
                vz[1][block, rows + hi : rows + hi + width, :],
            )
            bottom = is_own if h == 0 else jnp.logical_not(is_own)
            row = pl.multiple_of(jnp.where(bottom, total_rows - width, 0), width)
            halves.append((v, z, pl.ds(row, width)))
        edges = [x[h][halves[h][2], :] for h in range(2)]
        y = product(split(halves[0][1]), split(edges[0])) + product(split(halves[1][1]), split(edges[1]))
        y = split(pick(act, y, 0.0))
        for h in range(2):
            x[h][halves[h][2], :] = edges[h] - product(split(halves[h][0]), y)


def wave(ticks, first, last, state, vz, prev, msgs, offs, place, steps, inner, pairs, n_links):
    plan = (tuple(ticks), first, last, steps, inner, pairs, n_links)
    vmem = pl.BlockSpec(memory_space=pltpu.VMEM)
    smem = pl.BlockSpec(memory_space=pltpu.SMEM)
    arrays = list(state) + list(vz) + list(prev) + (list(msgs[0]) + list(msgs[1]) if first else [])
    width, cols = vz[0].shape[2], state[0].shape[1]
    shapes = [jax.ShapeDtypeStruct(s.shape, F32) for s in state]
    if last:
        shapes += [jax.ShapeDtypeStruct((width, cols), F32)] * n_links
    result = pl.pallas_call(
        functools.partial(wave_kernel, plan),
        in_specs=[smem, smem] + [vmem] * len(arrays),
        out_specs=[vmem] * len(shapes),
        out_shape=shapes,
        compiler_params=pltpu.CompilerParams(vmem_limit_bytes=24 * 1024 * 1024),
        name="wave",
    )(offs, place, *arrays)
    return result[:2], result[2:]


def per_device(vectors, reflectors, wy_factors, block_slots, offsets):
    n_row, n_col = lax.axis_size("row"), lax.axis_size("col")
    pairs = n_row // 2
    row = lax.axis_index("row")
    p, k = row // 2, row % 2
    steps, inner = offsets.shape[1], offsets.shape[2]
    rows, width = reflectors.shape[2:]
    half = vectors.shape[1] // 2
    n_y = 2 ** (int(math.log2(n_col)) // 2)
    swap = [(i, i ^ 1) for i in range(n_row)]

    mine = exchange_slots(reflectors[0], wy_factors[0], block_slots[0], n_col)
    left, right = vectors[:, :half], vectors[:, half:]
    own = jnp.where(k == 0, left, right)
    other = lax.ppermute(jnp.where(k == 0, right, left), "row", swap)
    offs_own = offsets[0].reshape(-1)
    offs_other = lax.ppermute(offs_own, "row", swap)
    offs = jnp.clip(jnp.stack([offs_own, offs_other]), 0, vectors.shape[0] - rows)
    place = jnp.stack([p, k]).astype(jnp.int32)

    found = gather_pieces(mine, n_col, n_y)
    vz_own, edge = prepare(found, rows, width, steps)
    vz_other = lax.ppermute(vz_own, "row", swap)
    above = lax.ppermute(edge, "row", [(i, i + 1) for i in range(1, n_row - 1, 2)])
    above_again = lax.ppermute(above, "row", [(i, i + 1) for i in range(0, n_row, 2)])

    n_links = 1 if pairs == 2 else 2
    last_tick = n_row + steps - 2
    stops = [
        t
        for t in range(last_tick + 1)
        if any(0 <= t - 2 * q - 1 < steps for q in range(pairs - 1))
    ]
    state, msgs, first, ticks = (own, other), None, False, []
    for t in range(last_tick + 1):
        ticks.append(t)
        last = t in stops
        if not last and t < last_tick:
            continue
        state, sent = wave(
            ticks, first, last, state, (vz_own, vz_other), (above, above_again), msgs, offs, place,
            steps, inner, pairs, n_links,
        )
        if last:
            if n_links == 1:
                got = [lax.ppermute(sent[0], "row", [(i, (i + 2) % 4) for i in range(4)])]
            else:
                got = [
                    lax.ppermute(sent[1], "row", [(i + 2, i) for i in range(n_row - 2)]),
                    lax.ppermute(sent[0], "row", [(i, i + 2) for i in range(n_row - 2)]),
                ]
            msgs = (sent, got)
        first, ticks = last, []
    own, other = state
    back = lax.ppermute(other, "row", swap)
    return jnp.where(k == 0, jnp.concatenate([own, back], 1), jnp.concatenate([back, own], 1))


def solution(mesh):
    in_specs = (
        P("row", "col"),
        P("row", "col", None, None),
        P("row", "col", None, None),
        P("row", None, None),
        P("row", None, None),
    )
    out_specs = P("row", "col")
    return jax.shard_map(
        per_device, mesh=mesh, in_specs=in_specs, out_specs=out_specs, check_vma=False
    )
```

time: 470 us -> 158 us (0.34)
  waiting for transfers between devices: 251 us -> 74.6 us
  between operations: 53.7 us -> 0.28 us
  starting transfers between devices: 77.7 us -> 36.2 us
  Pallas kernels: 0 us -> 31.7 us
  matrix products: 27.3 us -> 0 us
  loops' own time: 23.2 us -> 0 us
  local copies, waits for them, and re-layouts: 31 us -> 8.76 us
    psum x1 -> x0, waiting for transfers between devices: 144 us -> none  [spread(): return lax.psum(block, axis)]
    ppermute x20 -> x18, waiting for transfers between devices: 106 us -> 55.7 us  [the longest x4 25 us: spread_y(): sent = lax.ppermute(sent, 'col', turn)]
    ppermute x20 -> x18, starting transfers between devices: 77.7 us -> 30.7 us  [the longest x1 6.4 us: per_device(): offs_other = lax.ppermute(offs_own, 'row', swap)]
    pallas_call x0 -> x6, Pallas kernels: none -> 31.7 us  [the longest x5 25.4 us: wave(): pl.pallas_call(functools.partial(wave_kernel, plan), in_specs=[smem, smem...]
    dot_general x48 -> x0, matrix products: 27.3 us -> none  [the longest x16 16.8 us: reflect(): jnp.dot(factor, coeffs, precision=best, preferred_element_type=jnp.float32)]
    another operation x11 -> x0, loops' own time: 23.2 us -> none  [the longest x10 22.5 us: wave_tick(): lax.cond(active, lambda operands: advance(operands[0], operands[1], benea...]
    all_to_all x0 -> x1, waiting for transfers between devices: none -> 18.9 us  [exchange_slots(): parcels = lax.all_to_all(parcels, 'col', 0, 0, tiled=True)]
    unnamed x78 -> x24, local copies, waits for them, and re-layouts: 16.1 us -> 3.06 us
  transfers between devices with their start and end apart: 21 -> 19, of which waited for: 21 -> 14; matrix products, arithmetic and copies ran while one was open for 0% -> 4% of each run, Pallas kernels for 0% -> 0%
where the time goes in v1:
time: 158 us; the launch traced here: 156 us
  waiting for transfers between devices  74.6 us (47%)
  starting transfers between devices  36.2 us (23%)
  Pallas kernels  31.7 us (20%)
  local copies, waits for them, and re-layouts  8.76 us (6%)
  other arithmetic  4.9 us (3%)
    pallas_call x5, Pallas kernels, wave(): pl.pallas_call(functools.partial(wave_kernel, plan), in_specs=[smem, smem...  25.4 us
    ppermute x4, waiting for transfers between devices, spread_y(): sent = lax.ppermute(sent, 'col', turn)  25 us
    all_to_all x1, waiting for transfers between devices, exchange_slots(): parcels = lax.all_to_all(parcels, 'col', 0, 0, tiled=True)  18.9 us
    ppermute x4, waiting for transfers between devices, per_device(): got = [lax.ppermute(sent[0], 'row', [(i, (i + 2) % 4) for i in range(4)])]  12.5 us
    ppermute x1, waiting for transfers between devices, gather_pieces(): low = lax.ppermute(low, 'col', backward)  7.8 us
    ppermute x1, starting transfers between devices, per_device(): offs_other = lax.ppermute(offs_own, 'row', swap)  6.4 us
    pallas_call x1, Pallas kernels, prepare(): pl.pallas_call(functools.partial(prepare_kernel, rows, width), grid_spec=...  6.35 us
    all_to_all x1, starting transfers between devices, exchange_slots(): parcels = lax.all_to_all(parcels, 'col', 0, 0, tiled=True)  5.55 us
  transfers between devices with their start and end apart: 19, of which 14 were waited for; matrix products, arithmetic and copies ran while one was open for 4% of the time, Pallas kernels for 0%

profile of v1, /device:TPU:3, one launch (start us, length us, event | category | flops | bytes accessed | tf_op | source)
XLA Modules:
  0.0 156.5 jit_solution(10380856482027251525)
XLA Ops:
  0.0 1.2 maximum_bitcast_fusion
  1.2 0.9 copy.16
  2.1 5.6 %all-to-all-start = ((f32[8,4,48,128]{3,2,1,0:T(8,128)}), f32[8,4,48,128]{3,2,1,0:T(8,128)S(1)}, u32[]{:S(2)}, u32[]{:S(2)}) async-start(f32[8,4,48,128]{3,2,1,0:T(8,128)} %copy.16), calls=%async_computation | async-start | bytes 1572864 | tf_op jit(solution)/shard_map/all_to_all | solution.py:76
  7.7 0.1 min.28
  7.8 0.1 min.26
  7.9 18.9 %all-to-all-done = f32[8,4,48,128]{3,2,1,0:T(8,128)S(1)} async-done(((f32[8,4,48,128]{3,2,1,0:T(8,128)}), f32[8,4,48,128]{3,2,1,0:T(8,128)S(1)}, u32[]{:S(2)}, u32[]{:S(2)}) %all-to-all-start) | async-done | bytes 786464 | tf_op jit(solution)/shard_map/all_to_all | solution.py:76
  26.8 0.6 gather_fusion
  27.4 0.1 broadcast_select_fusion.refs_0_
  27.5 0.0 copy-start.1
  27.5 2.2 %collective-permute-start.2 = (f32[16,48,128]{2,1,0:T(8,128)S(1)}, f32[16,48,128]{2,1,0:T(8,128)S(1)}, u32[]{:S(2)}, u32[]{:S(2)}) collective-permute-start(f32[16,48,128]{2,1,0:T(8,128)S(1)} %broadcast_select_fusion.refs_0_), channel_id=1, source_target_pairs={{0,6},{1,7},{2,0},{3,1},{4,2},{5,3},{6,4},{7,5},{8,14},{9,15},{10,... | collective-permute-start | bytes 1179656 | tf_op jit(solution)/shard_map/ppermute | solution.py:60
  29.6 0.0 collective-permute-start.3
  29.7 7.8 %collective-permute-done.2.refs_1_ = f32[16,48,128]{2,1,0:T(8,128)S(1)} collective-permute-done((f32[16,48,128]{2,1,0:T(8,128)S(1)}, f32[16,48,128]{2,1,0:T(8,128)S(1)}, u32[]{:S(2)}, u32[]{:S(2)}) %collective-permute-start.2) | collective-permute-done | bytes 393248 | tf_op jit(solution)/shard_map/ppermute | solution.py:60
  37.5 4.1 %collective-permute-start.4 = (f32[8,48,128]{2,1,0:T(8,128)S(1)}, f32[8,48,128]{2,1,0:T(8,128)S(1)}, u32[]{:S(2)}, u32[]{:S(2)}) collective-permute-start(f32[8,48,128]{2,1,0:T(8,128)S(1)} %slice.18), channel_id=1, source_target_pairs={{0,6},{1,7},{2,0},{3,1},{4,2},{5,3},{6,4},{7,5},{8,14},{9,15},{10,... | collective-permute-start | bytes 589832 | tf_op jit(solution)/shard_map/ppermute | solution.py:55
  41.5 5.3 %collective-permute-done.3.refs_2_ = f32[16,48,128]{2,1,0:T(8,128)S(1)} collective-permute-done((f32[16,48,128]{2,1,0:T(8,128)S(1)}, f32[16,48,128]{2,1,0:T(8,128)S(1)}, u32[]{:S(2)}, u32[]{:S(2)}) %collective-permute-start.3) | collective-permute-done | bytes 393248 | tf_op jit(solution)/shard_map/ppermute | solution.py:61
  46.9 1.3 collective-permute-start.5
  48.2 1.9 %collective-permute-start.6 = (f32[16,48,128]{2,1,0:T(8,128)S(1)}, f32[16,48,128]{2,1,0:T(8,128)S(1)}, u32[]{:S(2)}, u32[]{:S(2)}) collective-permute-start(f32[16,48,128]{2,1,0:T(8,128)S(1)} %broadcast_select_fusion.refs_0_), channel_id=1, source_target_pairs={{0,1},{1,0},{2,3},{3,2},{4,5},{5,4},{6,7},{7,6},{8,9},{9,8},{10,11... | collective-permute-start | bytes 1179656 | tf_op jit(solution)/shard_map/ppermute | solution.py:41
  50.1 0.0 collective-permute-start.8
  50.1 1.4 collective-permute-start.7
  51.6 0.7 collective-permute-done.4
  52.3 2.1 %collective-permute-done.5 = f32[8,48,128]{2,1,0:T(8,128)S(1)} collective-permute-done((f32[8,48,128]{2,1,0:T(8,128)S(1)}, f32[8,48,128]{2,1,0:T(8,128)S(1)}, u32[]{:S(2)}, u32[]{:S(2)}) %collective-permute-start.5) | collective-permute-done | bytes 196640 | tf_op jit(solution)/shard_map/ppermute | solution.py:55
  54.4 2.0 %collective-permute-start.9 = (f32[16,48,128]{2,1,0:T(8,128)S(1)}, f32[16,48,128]{2,1,0:T(8,128)S(1)}, u32[]{:S(2)}, u32[]{:S(2)}) collective-permute-start(f32[16,48,128]{2,1,0:T(8,128)S(1)} %constant_dynamic-update-slice_fusion.refs_3_), channel_id=1, source_target_pairs={{0,1},{1,0},{2,3},{3,2},{4,5},{5,4},{6,7},{7,6},{8,9},{9,8},{10,11... | collective-permute-start | bytes 1179656 | tf_op jit(solution)/shard_map/ppermute | solution.py:41
  56.4 0.7 stack.55.sources
  57.1 0.0 collective-permute-done.6.refs_4_
  57.1 8.1 %collective-permute-done.8.refs_6_ = f32[16,48,128]{2,1,0:T(8,128)S(1)} collective-permute-done((f32[16,48,128]{2,1,0:T(8,128)S(1)}, f32[16,48,128]{2,1,0:T(8,128)S(1)}, u32[]{:S(2)}, u32[]{:S(2)}) %collective-permute-start.8) | collective-permute-done | bytes 393248 | tf_op jit(solution)/shard_map/ppermute | solution.py:41
  65.2 8.4 %collective-permute-done.7.refs_5_ = f32[16,48,128]{2,1,0:T(8,128)S(1)} collective-permute-done((f32[16,48,128]{2,1,0:T(8,128)S(1)}, f32[16,48,128]{2,1,0:T(8,128)S(1)}, u32[]{:S(2)}, u32[]{:S(2)}) %collective-permute-start.7) | collective-permute-done | bytes 393248 | tf_op jit(solution)/shard_map/ppermute | solution.py:41
  73.6 8.4 %collective-permute-done.9.refs_7_ = f32[16,48,128]{2,1,0:T(8,128)S(1)} collective-permute-done((f32[16,48,128]{2,1,0:T(8,128)S(1)}, f32[16,48,128]{2,1,0:T(8,128)S(1)}, u32[]{:S(2)}, u32[]{:S(2)}) %collective-permute-start.9) | collective-permute-done | bytes 393248 | tf_op jit(solution)/shard_map/ppermute | solution.py:41
  82.1 0.7 copy-done.8
  82.8 6.3 %prepare.1 = (f32[16,512,128]{2,1,0:T(8,128)}, f32[4,256,128]{2,1,0:T(8,128)}) custom-call(s32[8]{0:T(128)} %stack.55.sources, f32[16,48,128]{2,1,0:T(8,128)} %copy-done.1, f32[16,48,128]{2,1,0:T(8,128)} %copy-done.2, f32[16,48,128]{2,1,0:T(8,128)} %copy-done.3, f32[16,48,128]{2,1,0:T(8,128)} %copy-done.4, f32[16,48,128]{2,1,0:T(8,128)} %copy-done.5, ...), custom_call_target="tpu_custom_call" | custom-call | tf_op jit(solution)/shard_map/prepare/pallas_call | solution.py:124
  89.2 3.4 %collective-permute-start.10 = (f32[16,512,128]{2,1,0:T(8,128)}, f32[16,512,128]{2,1,0:T(8,128)}, u32[]{:S(2)}, u32[]{:S(2)}) collective-permute-start(f32[16,512,128]{2,1,0:T(8,128)} %get-tuple-element.21.refs_4_), channel_id=1, source_target_pairs={{0,8},{8,0},{16,24},{24,16},{1,9},{9,1},{17,25},{25,17},{2,10},{10... | collective-permute-start | bytes 12582920 | tf_op jit(solution)/shard_map/ppermute | solution.py:280
  92.6 0.7 collective-permute-start.11
  93.3 1.9 %slice_select_fusion = (f32[2048,64]{1,0:T(8,128)S(1)}, f32[2048,64]{1,0:T(8,128)S(1)}) fusion(f32[2048,128]{1,0:T(8,128)} %param.5, pred[]{:T(512)S(6)} %eq.19), kind=kLoop, calls=%fused_computation.2 | loop fusion | flops 262144 | bytes 2097153 | tf_op jit(solution)/shard_map/jit(_where)/select_n | solution.py:272
  95.2 1.1 copy.15
  96.4 0.6 collective-permute-start.1
  97.0 0.0 collective-permute-done.11.refs_6_
  97.0 1.5 collective-permute-start.12
  98.5 0.1 copy.13
  98.6 0.1 reshape_squeeze.10
  98.7 6.4 %collective-permute-start = (s32[12]{0:T(128)S(1)}, s32[12]{0:T(128)S(1)}, u32[]{:S(2)}, u32[]{:S(2)}) collective-permute-start(s32[12]{0:T(128)S(1)} %reshape_squeeze.10), channel_id=1, source_target_pairs={{0,8},{8,0},{16,24},{24,16},{1,9},{9,1},{17,25},{25,17},{2,10},{10... | collective-permute-start | bytes 152 | tf_op jit(solution)/shard_map/ppermute | solution.py:274
  105.1 0.1 stack_reshape_squeeze.3
  105.1 0.1 pad_add_fusion.refs_1_
  105.2 0.8 collective-permute-done
  106.0 0.0 collective-permute-done.1
  106.1 1.4 copy.17.refs_3_
  107.4 0.0 collective-permute-done.12.refs_7_
  107.4 0.0 collective-permute-done.10.refs_5_
  107.5 2.2 %copy-done = f32[16,512,128]{2,1,0:T(8,128)S(1)} copy-done((f32[16,512,128]{2,1,0:T(8,128)S(1)}, f32[16,512,128]{2,1,0:T(8,128)}, u32[]{:S(2)}) %copy-start) | copy-done | bytes 4194328
  109.6 6.1 %wave.5 = (f32[2048,64]{1,0:T(8,128)S(1)}, f32[2048,64]{1,0:T(8,128)S(1)}, f32[128,64]{1,0:T(8,128)S(1)}) custom-call(s32[2,12]{1,0:T(2,128)S(1)} %add_clamp_fusion.refs_0_, s32[2]{0:T(128)S(1)} %pad_add_fusion.refs_1_, f32[2048,64]{1,0:T(8,128)S(1)} %get-tuple-element.38.refs_2_, f32[2048,64]{1,0:T(8,128)S(1)} %copy.17.refs_3_, ...), custom_call_target="tpu_custom_call" | custom-call | tf_op jit(solution)/shard_map/wave/pallas_call | solution.py:247
  115.8 0.2 collective-permute-start.13
  115.9 3.4 %collective-permute-done.13.refs_9_ = f32[128,64]{1,0:T(8,128)S(1)} collective-permute-done((f32[128,64]{1,0:T(8,128)S(1)}, f32[128,64]{1,0:T(8,128)S(1)}, u32[]{:S(2)}, u32[]{:S(2)}) %collective-permute-start.13) | collective-permute-done | bytes 32800 | tf_op jit(solution)/shard_map/ppermute | solution.py:303
  119.3 4.4 %wave.6 = (f32[2048,64]{1,0:T(8,128)S(1)}, f32[2048,64]{1,0:T(8,128)S(1)}, f32[128,64]{1,0:T(8,128)S(1)}) custom-call(s32[2,12]{1,0:T(2,128)S(1)} %add_clamp_fusion.refs_0_, s32[2]{0:T(128)S(1)} %pad_add_fusion.refs_1_, f32[2048,64]{1,0:T(8,128)S(1)} %get-tuple-element.23.refs_2_, f32[2048,64]{1,0:T(8,128)S(1)} %get-tuple-element.24.refs_3_, ...), custom_call_target="tpu_custom_call" | custom-call | tf_op jit(solution)/shard_map/wave/pallas_call | solution.py:247
  123.7 0.1 collective-permute-start.14
  123.8 3.0 %collective-permute-done.14.refs_9_ = f32[128,64]{1,0:T(8,128)S(1)} collective-permute-done((f32[128,64]{1,0:T(8,128)S(1)}, f32[128,64]{1,0:T(8,128)S(1)}, u32[]{:S(2)}, u32[]{:S(2)}) %collective-permute-start.14) | collective-permute-done | bytes 32800 | tf_op jit(solution)/shard_map/ppermute | solution.py:303
  126.9 4.4 %wave.7 = (f32[2048,64]{1,0:T(8,128)S(1)}, f32[2048,64]{1,0:T(8,128)S(1)}, f32[128,64]{1,0:T(8,128)S(1)}) custom-call(s32[2,12]{1,0:T(2,128)S(1)} %add_clamp_fusion.refs_0_, s32[2]{0:T(128)S(1)} %pad_add_fusion.refs_1_, f32[2048,64]{1,0:T(8,128)S(1)} %get-tuple-element.26.refs_2_, f32[2048,64]{1,0:T(8,128)S(1)} %get-tuple-element.27.refs_3_, ...), custom_call_target="tpu_custom_call" | custom-call | tf_op jit(solution)/shard_map/wave/pallas_call | solution.py:247
  131.3 0.2 collective-permute-start.15
  131.4 3.0 %collective-permute-done.15.refs_9_ = f32[128,64]{1,0:T(8,128)S(1)} collective-permute-done((f32[128,64]{1,0:T(8,128)S(1)}, f32[128,64]{1,0:T(8,128)S(1)}, u32[]{:S(2)}, u32[]{:S(2)}) %collective-permute-start.15) | collective-permute-done | bytes 32800 | tf_op jit(solution)/shard_map/ppermute | solution.py:303
  134.5 4.4 %wave.8 = (f32[2048,64]{1,0:T(8,128)S(1)}, f32[2048,64]{1,0:T(8,128)S(1)}, f32[128,64]{1,0:T(8,128)S(1)}) custom-call(s32[2,12]{1,0:T(2,128)S(1)} %add_clamp_fusion.refs_0_, s32[2]{0:T(128)S(1)} %pad_add_fusion.refs_1_, f32[2048,64]{1,0:T(8,128)S(1)} %get-tuple-element.29.refs_2_, f32[2048,64]{1,0:T(8,128)S(1)} %get-tuple-element.30.refs_3_, ...), custom_call_target="tpu_custom_call" | custom-call | tf_op jit(solution)/shard_map/wave/pallas_call | solution.py:247
  138.9 0.1 collective-permute-start.16
  139.0 3.0 %collective-permute-done.16.refs_9_ = f32[128,64]{1,0:T(8,128)S(1)} collective-permute-done((f32[128,64]{1,0:T(8,128)S(1)}, f32[128,64]{1,0:T(8,128)S(1)}, u32[]{:S(2)}, u32[]{:S(2)}) %collective-permute-start.16) | collective-permute-done | bytes 32800 | tf_op jit(solution)/shard_map/ppermute | solution.py:303
  142.0 6.1 %wave.9 = (f32[2048,64]{1,0:T(8,128)S(1)}, f32[2048,64]{1,0:T(8,128)S(1)}) custom-call(s32[2,12]{1,0:T(2,128)S(1)} %add_clamp_fusion.refs_0_, s32[2]{0:T(128)S(1)} %pad_add_fusion.refs_1_, f32[2048,64]{1,0:T(8,128)S(1)} %get-tuple-element.32.refs_2_, f32[2048,64]{1,0:T(8,128)S(1)} %get-tuple-element.33.refs_3_, f32[16,512,128]{2,1,0:T(8,128)S(1)} %copy-done, ...), custom_call_target="tpu_custom_call" | custom-call | tf_op jit(solution)/shard_map/wave/pallas_call | solution.py:247
  148.1 0.3 copy.18
  148.5 4.5 %collective-permute-start.17 = (f32[2048,64]{0,1:T(8,128)S(1)}, f32[2048,64]{0,1:T(8,128)S(1)}, u32[]{:S(2)}, u32[]{:S(2)}) collective-permute-start(f32[2048,64]{0,1:T(8,128)S(1)} %copy.18), channel_id=1, source_target_pairs={{0,8},{8,0},{16,24},{24,16},{1,9},{9,1},{17,25},{25,17},{2,10},{10... | collective-permute-start | bytes 1572872 | tf_op jit(solution)/shard_map/ppermute | solution.py:312
  153.0 1.5 collective-permute-done.17
  154.6 0.3 copy.19
  154.9 1.6 %maximum_select_fusion = f32[2048,128]{1,0:T(8,128)} fusion(f32[2048,64]{1,0:T(8,128)S(1)} %copy.19, f32[2048,64]{1,0:T(8,128)S(1)} %get-tuple-element.35, pred[]{:T(512)S(6)} %eq.19), kind=kLoop, calls=%fused_computation.1 | loop fusion | flops 786432 | bytes 2097153 | tf_op jit(solution)/shard_map/jit(_where)/select_n | solution.py:313
  (28 shorter events, 0.1 us)
Async XLA Ops:
  0.0 7.7 %copy-start.9 = (s32[1,4,4]{2,1,0:T(4,128)S(1)}, s32[1,4,4]{2,1,0:T(4,128)}, u32[]{:S(2)}) copy-start(s32[1,4,4]{2,1,0:T(4,128)} %param.8) | copy-start | bytes 196
  2.1 24.6 %all-to-all-start = ((f32[8,4,48,128]{3,2,1,0:T(8,128)}), f32[8,4,48,128]{3,2,1,0:T(8,128)S(1)}, u32[]{:S(2)}, u32[]{:S(2)}) async-start(f32[8,4,48,128]{3,2,1,0:T(8,128)} %copy.16), calls=%async_computation | async-start | bytes 1572864 | tf_op jit(solution)/shard_map/all_to_all | solution.py:76
  27.5 54.6 %copy-start.1 = (f32[16,48,128]{2,1,0:T(8,128)}, f32[16,48,128]{2,1,0:T(8,128)S(1)}, u32[]{:S(2)}) copy-start(f32[16,48,128]{2,1,0:T(8,128)S(1)} %broadcast_select_fusion.refs_0_) | copy-start | bytes 1179652
  27.5 10.0 %collective-permute-start.2 = (f32[16,48,128]{2,1,0:T(8,128)S(1)}, f32[16,48,128]{2,1,0:T(8,128)S(1)}, u32[]{:S(2)}, u32[]{:S(2)}) collective-permute-start(f32[16,48,128]{2,1,0:T(8,128)S(1)} %broadcast_select_fusion.refs_0_), channel_id=1, source_target_pairs={{0,6},{1,7},{2,0},{3,1},{4,2},{5,3},{6,4},{7,5},{8,14},{9,15},{10,... | collective-permute-start | bytes 1179656 | tf_op jit(solution)/shard_map/ppermute | solution.py:60
  29.6 17.2 %collective-permute-start.3 = (f32[16,48,128]{2,1,0:T(8,128)S(1)}, f32[16,48,128]{2,1,0:T(8,128)S(1)}, u32[]{:S(2)}, u32[]{:S(2)}) collective-permute-start(f32[16,48,128]{2,1,0:T(8,128)S(1)} %broadcast_select_fusion.refs_0_), channel_id=1, source_target_pairs={{0,2},{1,3},{2,4},{3,5},{4,6},{5,7},{6,0},{7,1},{8,10},{9,11},{10,... | collective-permute-start | bytes 1179656 | tf_op jit(solution)/shard_map/ppermute | solution.py:61
  37.5 44.6 %copy-start.2 = (f32[16,48,128]{2,1,0:T(8,128)}, f32[16,48,128]{2,1,0:T(8,128)S(1)}, u32[]{:S(2)}) copy-start(f32[16,48,128]{2,1,0:T(8,128)S(1)} %collective-permute-done.2.refs_1_) | copy-start | bytes 1179652
  37.5 14.8 %collective-permute-start.4 = (f32[8,48,128]{2,1,0:T(8,128)S(1)}, f32[8,48,128]{2,1,0:T(8,128)S(1)}, u32[]{:S(2)}, u32[]{:S(2)}) collective-permute-start(f32[8,48,128]{2,1,0:T(8,128)S(1)} %slice.18), channel_id=1, source_target_pairs={{0,6},{1,7},{2,0},{3,1},{4,2},{5,3},{6,4},{7,5},{8,14},{9,15},{10,... | collective-permute-start | bytes 589832 | tf_op jit(solution)/shard_map/ppermute | solution.py:55
  46.9 35.2 %copy-start.3 = (f32[16,48,128]{2,1,0:T(8,128)}, f32[16,48,128]{2,1,0:T(8,128)S(1)}, u32[]{:S(2)}) copy-start(f32[16,48,128]{2,1,0:T(8,128)S(1)} %collective-permute-done.3.refs_2_) | copy-start | bytes 1179652
  46.9 7.5 %collective-permute-start.5 = (f32[8,48,128]{2,1,0:T(8,128)S(1)}, f32[8,48,128]{2,1,0:T(8,128)S(1)}, u32[]{:S(2)}, u32[]{:S(2)}) collective-permute-start(f32[8,48,128]{2,1,0:T(8,128)S(1)} %slice.19), channel_id=1, source_target_pairs={{0,2},{1,3},{2,4},{3,5},{4,6},{5,7},{6,0},{7,1},{8,10},{9,11},{10,... | collective-permute-start | bytes 589832 | tf_op jit(solution)/shard_map/ppermute | solution.py:55
  48.2 8.9 %collective-permute-start.6 = (f32[16,48,128]{2,1,0:T(8,128)S(1)}, f32[16,48,128]{2,1,0:T(8,128)S(1)}, u32[]{:S(2)}, u32[]{:S(2)}) collective-permute-start(f32[16,48,128]{2,1,0:T(8,128)S(1)} %broadcast_select_fusion.refs_0_), channel_id=1, source_target_pairs={{0,1},{1,0},{2,3},{3,2},{4,5},{5,4},{6,7},{7,6},{8,9},{9,8},{10,11... | collective-permute-start | bytes 1179656 | tf_op jit(solution)/shard_map/ppermute | solution.py:41
  50.1 15.1 %collective-permute-start.8 = (f32[16,48,128]{2,1,0:T(8,128)S(1)}, f32[16,48,128]{2,1,0:T(8,128)S(1)}, u32[]{:S(2)}, u32[]{:S(2)}) collective-permute-start(f32[16,48,128]{2,1,0:T(8,128)S(1)} %collective-permute-done.3.refs_2_), channel_id=1, source_target_pairs={{0,1},{1,0},{2,3},{3,2},{4,5},{5,4},{6,7},{7,6},{8,9},{9,8},{10,11... | collective-permute-start | bytes 1179656 | tf_op jit(solution)/shard_map/ppermute | solution.py:41
  50.1 23.5 %collective-permute-start.7 = (f32[16,48,128]{2,1,0:T(8,128)S(1)}, f32[16,48,128]{2,1,0:T(8,128)S(1)}, u32[]{:S(2)}, u32[]{:S(2)}) collective-permute-start(f32[16,48,128]{2,1,0:T(8,128)S(1)} %collective-permute-done.2.refs_1_), channel_id=1, source_target_pairs={{0,1},{1,0},{2,3},{3,2},{4,5},{5,4},{6,7},{7,6},{8,9},{9,8},{10,11... | collective-permute-start | bytes 1179656 | tf_op jit(solution)/shard_map/ppermute | solution.py:41
  54.4 27.7 %copy-start.4 = (f32[16,48,128]{2,1,0:T(8,128)}, f32[16,48,128]{2,1,0:T(8,128)S(1)}, u32[]{:S(2)}) copy-start(f32[16,48,128]{2,1,0:T(8,128)S(1)} %constant_dynamic-update-slice_fusion.refs_3_) | copy-start | bytes 1179652
  54.4 27.7 %collective-permute-start.9 = (f32[16,48,128]{2,1,0:T(8,128)S(1)}, f32[16,48,128]{2,1,0:T(8,128)S(1)}, u32[]{:S(2)}, u32[]{:S(2)}) collective-permute-start(f32[16,48,128]{2,1,0:T(8,128)S(1)} %constant_dynamic-update-slice_fusion.refs_3_), channel_id=1, source_target_pairs={{0,1},{1,0},{2,3},{3,2},{4,5},{5,4},{6,7},{7,6},{8,9},{9,8},{10,11... | collective-permute-start | bytes 1179656 | tf_op jit(solution)/shard_map/ppermute | solution.py:41
  57.1 41.4 %copy-start.10 = (s32[1,4,3]{1,0,2:T(1,128)S(1)}, s32[1,4,3]{1,0,2:T(1,128)}, u32[]{:S(2)}) copy-start(s32[1,4,3]{1,0,2:T(1,128)} %param.9) | copy-start | bytes 148
  57.1 25.0 %copy-start.5 = (f32[16,48,128]{2,1,0:T(8,128)}, f32[16,48,128]{2,1,0:T(8,128)S(1)}, u32[]{:S(2)}) copy-start(f32[16,48,128]{2,1,0:T(8,128)S(1)} %collective-permute-done.6.refs_4_) | copy-start | bytes 1179652
  65.2 16.9 %copy-start.6 = (f32[16,48,128]{2,1,0:T(8,128)}, f32[16,48,128]{2,1,0:T(8,128)S(1)}, u32[]{:S(2)}) copy-start(f32[16,48,128]{2,1,0:T(8,128)S(1)} %collective-permute-done.8.refs_6_) | copy-start | bytes 1179652
  73.6 8.5 %copy-start.7 = (f32[16,48,128]{2,1,0:T(8,128)}, f32[16,48,128]{2,1,0:T(8,128)S(1)}, u32[]{:S(2)}) copy-start(f32[16,48,128]{2,1,0:T(8,128)S(1)} %collective-permute-done.7.refs_5_) | copy-start | bytes 1179652
  82.1 0.7 copy-start.8
  89.2 18.3 %collective-permute-start.10 = (f32[16,512,128]{2,1,0:T(8,128)}, f32[16,512,128]{2,1,0:T(8,128)}, u32[]{:S(2)}, u32[]{:S(2)}) collective-permute-start(f32[16,512,128]{2,1,0:T(8,128)} %get-tuple-element.21.refs_4_), channel_id=1, source_target_pairs={{0,8},{8,0},{16,24},{24,16},{1,9},{9,1},{17,25},{25,17},{2,10},{10... | collective-permute-start | bytes 12582920 | tf_op jit(solution)/shard_map/ppermute | solution.py:280
  92.6 4.4 %collective-permute-start.11 = (f32[4,256,128]{2,1,0:T(8,128)}, f32[4,256,128]{2,1,0:T(8,128)S(1)}, u32[]{:S(2)}, u32[]{:S(2)}) collective-permute-start(f32[4,256,128]{2,1,0:T(8,128)} %get-tuple-element.22), channel_id=1, source_target_pairs={{8,16},{9,17},{10,18},{11,19},{12,20},{13,21},{14,22},{15,23}} | collective-permute-start | bytes 1572872 | tf_op jit(solution)/shard_map/ppermute | solution.py:281
  96.4 9.7 %collective-permute-start.1 = (f32[2048,64]{0,1:T(8,128)}, f32[2048,64]{0,1:T(8,128)}, u32[]{:S(2)}, u32[]{:S(2)}) collective-permute-start(f32[2048,64]{0,1:T(8,128)} %copy.15), channel_id=1, source_target_pairs={{0,8},{8,0},{16,24},{24,16},{1,9},{9,1},{17,25},{25,17},{2,10},{10... | collective-permute-start | bytes 1572872 | tf_op jit(solution)/shard_map/ppermute | solution.py:272
  97.0 10.4 %collective-permute-start.12 = (f32[4,256,128]{2,1,0:T(8,128)S(1)}, f32[4,256,128]{2,1,0:T(8,128)S(1)}, u32[]{:S(2)}, u32[]{:S(2)}) collective-permute-start(f32[4,256,128]{2,1,0:T(8,128)S(1)} %collective-permute-done.11.refs_6_), channel_id=1, source_target_pairs={{0,8},{16,24},{1,9},{17,25},{2,10},{18,26},{3,11},{19,27},{4,12},{... | collective-permute-start | bytes 1572872 | tf_op jit(solution)/shard_map/ppermute | solution.py:282
  98.7 7.4 %collective-permute-start = (s32[12]{0:T(128)S(1)}, s32[12]{0:T(128)S(1)}, u32[]{:S(2)}, u32[]{:S(2)}) collective-permute-start(s32[12]{0:T(128)S(1)} %reshape_squeeze.10), channel_id=1, source_target_pairs={{0,8},{8,0},{16,24},{24,16},{1,9},{9,1},{17,25},{25,17},{2,10},{10... | collective-permute-start | bytes 152 | tf_op jit(solution)/shard_map/ppermute | solution.py:274
  107.5 2.2 %copy-start = (f32[16,512,128]{2,1,0:T(8,128)S(1)}, f32[16,512,128]{2,1,0:T(8,128)}, u32[]{:S(2)}) copy-start(f32[16,512,128]{2,1,0:T(8,128)} %get-tuple-element.21.refs_4_) | copy-start | bytes 12582916
  115.8 3.5 %collective-permute-start.13 = (f32[128,64]{1,0:T(8,128)S(1)}, f32[128,64]{1,0:T(8,128)S(1)}, u32[]{:S(2)}, u32[]{:S(2)}) collective-permute-start(f32[128,64]{1,0:T(8,128)S(1)} %get-tuple-element.25.refs_8_), channel_id=1, source_target_pairs={{0,16},{8,24},{16,0},{24,8},{1,17},{9,25},{17,1},{25,9},{2,18},{10... | collective-permute-start | bytes 98312 | tf_op jit(solution)/shard_map/ppermute | solution.py:303
  123.7 3.2 %collective-permute-start.14 = (f32[128,64]{1,0:T(8,128)S(1)}, f32[128,64]{1,0:T(8,128)S(1)}, u32[]{:S(2)}, u32[]{:S(2)}) collective-permute-start(f32[128,64]{1,0:T(8,128)S(1)} %get-tuple-element.28.refs_8_), channel_id=1, source_target_pairs={{0,16},{8,24},{16,0},{24,8},{1,17},{9,25},{17,1},{25,9},{2,18},{10... | collective-permute-start | bytes 98312 | tf_op jit(solution)/shard_map/ppermute | solution.py:303
  131.3 3.2 %collective-permute-start.15 = (f32[128,64]{1,0:T(8,128)S(1)}, f32[128,64]{1,0:T(8,128)S(1)}, u32[]{:S(2)}, u32[]{:S(2)}) collective-permute-start(f32[128,64]{1,0:T(8,128)S(1)} %get-tuple-element.31.refs_8_), channel_id=1, source_target_pairs={{0,16},{8,24},{16,0},{24,8},{1,17},{9,25},{17,1},{25,9},{2,18},{10... | collective-permute-start | bytes 98312 | tf_op jit(solution)/shard_map/ppermute | solution.py:303
  138.9 3.2 %collective-permute-start.16 = (f32[128,64]{1,0:T(8,128)S(1)}, f32[128,64]{1,0:T(8,128)S(1)}, u32[]{:S(2)}, u32[]{:S(2)}) collective-permute-start(f32[128,64]{1,0:T(8,128)S(1)} %get-tuple-element.34.refs_8_), channel_id=1, source_target_pairs={{0,16},{8,24},{16,0},{24,8},{1,17},{9,25},{17,1},{25,9},{2,18},{10... | collective-permute-start | bytes 98312 | tf_op jit(solution)/shard_map/ppermute | solution.py:303
  148.5 6.1 %collective-permute-start.17 = (f32[2048,64]{0,1:T(8,128)S(1)}, f32[2048,64]{0,1:T(8,128)S(1)}, u32[]{:S(2)}, u32[]{:S(2)}) collective-permute-start(f32[2048,64]{0,1:T(8,128)S(1)} %copy.18), channel_id=1, source_target_pairs={{0,8},{8,0},{16,24},{24,16},{1,9},{9,1},{17,25},{25,17},{2,10},{10... | collective-permute-start | bytes 1572872 | tf_op jit(solution)/shard_map/ppermute | solution.py:312
